TPU v7x, 512 devices: a whole 4x4x16 slice. The times are simulated.
512 devices in a mesh: dp: 32 (over z, core), member: 16 (over y, x).
Axes of the slice: x: 4, y: 4, z: 16, core: 2. Of those that a mesh axis runs over, the one named last changes fastest.
Arguments:
- tokens: bfloat16 [4096, 4096], P('dp', 'member'), may hold values from -6 to 6
- routes: int32 [4096, 2], P('dp'), may hold values from 0 to 7, all different within a row; in each aligned block of 128 rows (0 to 127, 128 to 255, ...) at most 34 rows name the same one
- route_weights: float32 [4096, 2], P('dp'), may hold values from 0.2 to 1
- up_stacked: bfloat16 [8, 4096, 7168], P(None, ('member', 'dp')), may hold values from -0.09375 to 0.09375
- down_stacked: bfloat16 [8, 4096, 7168], P(None, ('member', 'dp')), may hold values from -0.0625 to 0.0625
- cotangent: bfloat16 [4096, 4096], P('dp', 'member'), may hold values from -6 to 6
Outputs:
- mixed: bfloat16 [4096, 4096], P('dp', 'member')
- grad_tokens: bfloat16 [4096, 4096], P('dp', 'member')
- grad_up: bfloat16 [32, 4096, 1792], P('dp', 'member')
- grad_down: bfloat16 [32, 4096, 1792], P('dp', 'member')
Inputs may be any that keep to these rules, and one draw needn't show every extreme that they name: `routes`: each row names two different experts. In each aligned block of 128 rows no expert is named by more than 34 rows, and in some block some expert is named by exactly 34 rows.
All inputs are finite; a program needn't handle non-finite values.
Results may differ from a plain program's by a relative error of at most 0.018.
Values may be sent and summed in bfloat16 or wider, within the bound.
A program may use at most 64 MiB of HBM per device.

v0:
```python
import jax
import jax.numpy as jnp
from jax import lax
from jax.sharding import PartitionSpec as P

FF_W = 7168
E = 8
CAP = 34


def contract(left, right, left_dim, right_dim):
    return lax.dot_general(
        left, right, (((left_dim,), (right_dim,)), ((), ())), preferred_element_type=jnp.float32
    )


def body(tokens, routes, route_weights, up_stacked, down_stacked, cotangent):
    dp_count = lax.axis_size("dp")
    member_count = lax.axis_size("member")
    quarters = dp_count // E
    share_rows = up_stacked.shape[1]
    features = tokens.shape[1]
    hidden_own = FF_W // quarters
    per_member = hidden_own // member_count
    slots_all = E * CAP
    up_parts = (
        up_stacked.reshape(E, share_rows, quarters, hidden_own)
        .transpose(0, 2, 1, 3)
        .reshape(dp_count, share_rows, hidden_own)
    )
    down_parts = (
        down_stacked.reshape(E, share_rows, quarters, hidden_own)
        .transpose(0, 2, 1, 3)
        .reshape(dp_count, share_rows, hidden_own)
    )
    up_own, down_own = (
        lax.all_to_all(up_parts, "dp", split_axis=0, concat_axis=1, tiled=True),
        lax.all_to_all(down_parts, "dp", split_axis=0, concat_axis=1, tiled=True),
    )
    up_own = up_own.reshape(dp_count * share_rows, hidden_own)
    down_own = down_own.reshape(dp_count * share_rows, hidden_own)
    chosen = jnp.sum(
        (routes[:, :, None] == jnp.arange(E, dtype=jnp.int32)[None, None, :]).astype(jnp.float32),
        axis=1,
    )
    rows = jnp.arange(routes.shape[0], dtype=jnp.int32)
    earlier = (rows[None, :] < rows[:, None]).astype(jnp.bfloat16)
    before = jnp.dot(
        earlier, chosen.astype(jnp.bfloat16), preferred_element_type=jnp.float32
    ).astype(jnp.int32)
    slot_pos = jnp.sum(
        jnp.where(
            routes[:, :, None] == jnp.arange(E, dtype=jnp.int32)[None, None, :],
            before[:, None, :],
            0,
        ),
        axis=2,
    )
    target = routes * CAP + slot_pos
    slot_hits = jnp.arange(slots_all, dtype=jnp.int32)[:, None, None] == target[None, :, :]
    pick_table = jnp.sum(slot_hits.astype(jnp.float32), axis=2)
    weighted = jnp.sum(jnp.where(slot_hits, route_weights[None, :, :], 0.0), axis=2)
    x_local = jnp.dot(
        pick_table.astype(jnp.bfloat16), tokens, preferred_element_type=jnp.float32
    ).astype(jnp.bfloat16)
    d_local = jnp.dot(
        weighted, cotangent.astype(jnp.float32), precision=lax.Precision.HIGHEST
    ).astype(jnp.bfloat16)

    def spread(local):
        return jnp.broadcast_to(
            local.reshape(E, 1, CAP, features), (E, quarters, CAP, features)
        ).reshape(dp_count, CAP, features)

    def collect(returned):
        return jnp.sum(returned.reshape(E, quarters, CAP, features), axis=1).reshape(
            slots_all, features
        )

    x_in = lax.all_to_all(spread(x_local), "dp", split_axis=0, concat_axis=0, tiled=True).reshape(
        dp_count * CAP, features
    )
    partial_value = jnp.dot(x_in, up_own, preferred_element_type=jnp.float32).astype(jnp.bfloat16)
    pre_full = lax.psum(partial_value, "member").astype(jnp.float32)
    act_full = jax.nn.silu(pre_full).astype(jnp.bfloat16)
    y_part = contract(act_full, down_own, 1, 1)
    y_part, pre_full, act_full = (y_part, pre_full, act_full)
    y_back = lax.all_to_all(
        y_part.reshape(dp_count, CAP, features).astype(jnp.bfloat16),
        "dp",
        split_axis=0,
        concat_axis=0,
        tiled=True,
    ).astype(jnp.float32)
    d_in = lax.all_to_all(spread(d_local), "dp", split_axis=0, concat_axis=0, tiled=True).reshape(
        dp_count * CAP, features
    )
    d_act = lax.psum_scatter(
        contract(down_own, d_in, 0, 1).astype(jnp.bfloat16),
        "member",
        scatter_dimension=0,
        tiled=True,
    ).astype(jnp.float32)
    own_start = lax.axis_index("member") * per_member
    pre_share = lax.dynamic_slice_in_dim(pre_full, own_start, per_member, 1).T
    sigma = jax.nn.sigmoid(pre_share)
    d_share = (d_act * sigma * (1.0 + pre_share * (1.0 - sigma))).astype(jnp.bfloat16)
    d_pre = lax.all_gather(d_share, "member", axis=0, tiled=True)
    g_down = contract(d_in, act_full, 0, 0)
    g_up = contract(x_in, d_pre, 0, 1)
    dx_part = contract(d_pre, up_own, 0, 1)
    dx_part, g_up, g_down = (dx_part, g_up, g_down)
    dx_back = lax.all_to_all(
        dx_part.reshape(dp_count, CAP, features).astype(jnp.bfloat16),
        "dp",
        split_axis=0,
        concat_axis=0,
        tiled=True,
    ).astype(jnp.float32)
    y_slots = collect(y_back)
    dx_slots = collect(dx_back)
    mixed = jnp.dot(weighted.T, y_slots, precision=lax.Precision.HIGHEST).astype(jnp.bfloat16)
    grad_tokens = jnp.dot(pick_table.T, dx_slots, precision=lax.Precision.HIGHEST).astype(
        jnp.bfloat16
    )
    grad_up = g_up.astype(jnp.bfloat16).reshape(1, features, hidden_own)
    grad_down = g_down.astype(jnp.bfloat16).reshape(1, features, hidden_own)
    return (mixed, grad_tokens, grad_up, grad_down)


def solution(mesh):
    placed = (
        P("dp", "member"),
        P("dp", None),
        P("dp", None),
        P(None, ("member", "dp"), None),
        P(None, ("member", "dp"), None),
        P("dp", "member"),
    )
    return jax.shard_map(
        body,
        mesh=mesh,
        in_specs=placed,
        out_specs=(
            P("dp", "member"),
            P("dp", "member"),
            P("dp", "member", None),
            P("dp", "member", None),
        ),
        check_vma=False,
    )
```

profile of v0, /device:TPU:1, one launch (start us, length us, event | category | flops | bytes accessed | tf_op | source)
XLA Modules:
  0.0 533.1 jit_solution(2647584153746447925)
XLA Ops:
  11.4 16.7 %all-to-all-start.4 = ((bf16[32,34,256]{2,1,0:T(8,128)(2,1)}), bf16[32,34,256]{2,1,0:T(8,128)(2,1)S(1)}, u32[]{:S(2)}, u32[]{:S(2)}) async-start(bf16[32,34,256]{2,1,0:T(8,128)(2,1)} %bitcast.7), calls=%async_computation.4 | async-start | bytes 1310720 | tf_op jit(solution)/shard_map/all_to_all | solution.py:95
  29.2 38.0 %all-to-all-done.4 = bf16[32,34,256]{2,1,0:T(8,128)(2,1)S(1)} async-done(((bf16[32,34,256]{2,1,0:T(8,128)(2,1)}), bf16[32,34,256]{2,1,0:T(8,128)(2,1)S(1)}, u32[]{:S(2)}, u32[]{:S(2)}) %all-to-all-start.4) | async-done | bytes 557088 | tf_op jit(solution)/shard_map/all_to_all | solution.py:95
  68.1 4.1 all-to-all-start
  72.2 1.3 fusion.14
  74.6 36.7 %all-to-all-done = bf16[32,34,256]{2,1,0:T(8,128)(2,1)S(1)} async-done(((bf16[32,34,256]{2,1,0:T(8,128)(2,1)}), bf16[32,34,256]{2,1,0:T(8,128)(2,1)S(1)}, u32[]{:S(2)}, u32[]{:S(2)}) %all-to-all-start) | async-done | bytes 557088 | tf_op jit(solution)/shard_map/all_to_all | solution.py:80
  112.1 4.5 all-to-all-start.2
  116.6 1.3 fusion.15
  118.9 47.9 %all-to-all-done.2 = bf16[32,8,1792]{2,1,0:T(8,128)(2,1)S(1)} async-done(((bf16[32,8,1792]{2,1,0:T(8,128)(2,1)}), bf16[32,8,1792]{2,1,0:T(8,128)(2,1)S(1)}, u32[]{:S(2)}, u32[]{:S(2)}) %all-to-all-start.2) | async-done | bytes 917536 | tf_op jit(solution)/shard_map/all_to_all | solution.py:38
  166.9 4.5 all-to-all-start.1
  172.4 1.3 reshape.79
  173.7 4.4 convolution_convert_fusion
  178.1 6.4 %copy.27 = bf16[1792,1088]{0,1:T(8,128)(2,1)} copy(bf16[1792,1088]{1,0:T(8,128)(2,1)} %convolution_convert_fusion) | data formatting | bytes 7798784 | tf_op jit(solution)/shard_map/convert_element_type | solution.py:99
  184.5 37.2 %all-to-all-done.1 = bf16[32,8,1792]{2,1,0:T(8,128)(2,1)S(1)} async-done(((bf16[32,8,1792]{2,1,0:T(8,128)(2,1)}), bf16[32,8,1792]{2,1,0:T(8,128)(2,1)S(1)}, u32[]{:S(2)}, u32[]{:S(2)}) %all-to-all-start.1) | async-done | bytes 917536 | tf_op jit(solution)/shard_map/all_to_all | solution.py:37
  221.7 3.1 convolution_convert_fusion.1
  224.9 1.3 dynamic-slice
  226.8 156.5 %all-reduce.4.cloned.1.call-done = (bf16[1088,1792]{1,0:T(8,128)(2,1)}, bf16[1792,1088]{0,1:T(8,128)(2,1)}) async-done(((bf16[1088,1792]{1,0:T(8,128)(2,1)}, bf16[1792,1088]{0,1:T(8,128)(2,1)}), (bf16[1088,1792]{1,0:T(8,128)(2,1)}, bf16[1792,1088]{0,1:T(8,128)(2,1)})) %all-reduce.4.cloned.1.call-update) | async-done | bytes 7798800 | tf_op jit(solution)/shard_map/psum | solution.py:84
  383.3 2.7 convert_element_type.68
  385.9 1.4 fusion.11
  388.3 5.0 multiply_convert_fusion
  393.3 6.9 %dot_general.42 = bf16[32,34,1792]{2,1,0:T(8,128)(2,1)} reshape(bf16[1088,1792]{1,0:T(8,128)(2,1)} %multiply_convert_fusion) | data formatting | bytes 7798784 | tf_op jit(solution)/shard_map/dot_general | solution.py:12
  400.3 4.6 convolution_convert_fusion.5
  404.8 13.0 %all-to-all-start.3 = ((bf16[32,34,256]{2,1,0:T(8,128)(2,1)}), bf16[32,34,256]{2,1,0:T(8,128)(2,1)S(1)}, u32[]{:S(2)}, u32[]{:S(2)}) async-start(bf16[32,34,256]{2,1,0:T(8,128)(2,1)} %convolution_convert_fusion.5), calls=%async_computation.3 | async-start | bytes 1310720 | tf_op jit(solution)/shard_map/all_to_all | solution.py:88
  417.9 37.0 %all-gather.2.cloned.1.call-done = bf16[1792,1088]{1,0:T(8,128)(2,1)} async-done(((bf16[112,1088]{1,0:T(8,128)(2,1)}), bf16[1792,1088]{1,0:T(8,128)(2,1)}) %all-gather.2.cloned.1.call-update) | async-done | bytes 3899408 | tf_op jit(solution)/shard_map/all_gather | solution.py:108
  454.9 6.4 %copy.29 = bf16[1088,1792]{1,0:T(8,128)(2,1)} copy(bf16[1088,1792]{0,1:T(8,128)(2,1)} %bitcast.65) | data formatting | bytes 7798784 | tf_op jit(solution)/shard_map/dot_general | solution.py:12
  461.3 6.9 %dot_general.48 = bf16[32,34,1792]{2,1,0:T(8,128)(2,1)} reshape(bf16[1088,1792]{1,0:T(8,128)(2,1)} %copy.29) | data formatting | bytes 7798784 | tf_op jit(solution)/shard_map/dot_general | solution.py:12
  468.2 4.7 convolution_convert_fusion.4
  472.9 13.0 %all-to-all-start.5 = ((bf16[32,34,256]{2,1,0:T(8,128)(2,1)}), bf16[32,34,256]{2,1,0:T(8,128)(2,1)S(1)}, u32[]{:S(2)}, u32[]{:S(2)}) async-start(bf16[32,34,256]{2,1,0:T(8,128)(2,1)} %convolution_convert_fusion.4), calls=%async_computation.5 | async-start | bytes 1310720 | tf_op jit(solution)/shard_map/all_to_all | solution.py:113
  485.9 4.4 fusion.1
  490.5 1.1 convolution_convert_fusion.9
  491.6 4.5 fusion
  496.2 28.9 %all-to-all-done.5 = bf16[32,34,256]{2,1,0:T(8,128)(2,1)S(1)} async-done(((bf16[32,34,256]{2,1,0:T(8,128)(2,1)}), bf16[32,34,256]{2,1,0:T(8,128)(2,1)S(1)}, u32[]{:S(2)}, u32[]{:S(2)}) %all-to-all-start.5) | async-done | bytes 557088 | tf_op jit(solution)/shard_map/all_to_all | solution.py:113
  525.2 1.1 convolution_convert_fusion.8
  (32 shorter events, 11.2 us)
Async XLA Ops:
  7.2 3.0 copy-start
  11.4 55.9 %all-to-all-start.4 = ((bf16[32,34,256]{2,1,0:T(8,128)(2,1)}), bf16[32,34,256]{2,1,0:T(8,128)(2,1)S(1)}, u32[]{:S(2)}, u32[]{:S(2)}) async-start(bf16[32,34,256]{2,1,0:T(8,128)(2,1)} %bitcast.7), calls=%async_computation.4 | async-start | bytes 1310720 | tf_op jit(solution)/shard_map/all_to_all | solution.py:95
  68.1 43.1 %all-to-all-start = ((bf16[32,34,256]{2,1,0:T(8,128)(2,1)}), bf16[32,34,256]{2,1,0:T(8,128)(2,1)S(1)}, u32[]{:S(2)}, u32[]{:S(2)}) async-start(bf16[32,34,256]{2,1,0:T(8,128)(2,1)} %bitcast), calls=%async_computation | async-start | bytes 1310720 | tf_op jit(solution)/shard_map/all_to_all | solution.py:80
  111.3 0.8 copy-start.2
  112.1 54.7 %all-to-all-start.2 = ((bf16[32,8,1792]{2,1,0:T(8,128)(2,1)}), bf16[32,8,1792]{2,1,0:T(8,128)(2,1)S(1)}, u32[]{:S(2)}, u32[]{:S(2)}) async-start(bf16[32,8,1792]{2,1,0:T(8,128)(2,1)} %bitcast.3), calls=%async_computation.2 | async-start | bytes 1835008 | tf_op jit(solution)/shard_map/all_to_all | solution.py:38
  166.9 54.8 %all-to-all-start.1 = ((bf16[32,8,1792]{2,1,0:T(8,128)(2,1)}), bf16[32,8,1792]{2,1,0:T(8,128)(2,1)S(1)}, u32[]{:S(2)}, u32[]{:S(2)}) async-start(bf16[32,8,1792]{2,1,0:T(8,128)(2,1)} %bitcast.1), calls=%async_computation.1 | async-start | bytes 1835008 | tf_op jit(solution)/shard_map/all_to_all | solution.py:37
  171.4 211.8 %all-reduce.4.cloned.1.call-start = ((), (), s32[]{:S(2)}) async-start(), calls=%async_computation.7 | async-start | bytes 15597568 | tf_op jit(solution)/shard_map/psum | solution.py:84
  224.8 230.1 %all-gather.2.cloned.1.call-start = ((), (), s32[]{:S(2)}) async-start(), calls=%async_computation.6 | async-start | bytes 4386816 | tf_op jit(solution)/shard_map/all_gather | solution.py:108
  404.8 68.1 %all-to-all-start.3 = ((bf16[32,34,256]{2,1,0:T(8,128)(2,1)}), bf16[32,34,256]{2,1,0:T(8,128)(2,1)S(1)}, u32[]{:S(2)}, u32[]{:S(2)}) async-start(bf16[32,34,256]{2,1,0:T(8,128)(2,1)} %convolution_convert_fusion.5), calls=%async_computation.3 | async-start | bytes 1310720 | tf_op jit(solution)/shard_map/all_to_all | solution.py:88
  468.2 17.7 %copy-start.3 = (bf16[1088,256]{1,0:T(8,128)(2,1)S(1)}, bf16[1088,256]{1,0:T(8,128)(2,1)}, u32[]{:S(2)}) copy-start(bf16[1088,256]{1,0:T(8,128)(2,1)} %reshape.88) | copy-start | bytes 1671172
  472.9 52.1 %all-to-all-start.5 = ((bf16[32,34,256]{2,1,0:T(8,128)(2,1)}), bf16[32,34,256]{2,1,0:T(8,128)(2,1)S(1)}, u32[]{:S(2)}, u32[]{:S(2)}) async-start(bf16[32,34,256]{2,1,0:T(8,128)(2,1)} %convolution_convert_fusion.4), calls=%async_computation.5 | async-start | bytes 1310720 | tf_op jit(solution)/shard_map/all_to_all | solution.py:113
  490.5 35.8 %copy-start.1 = (bf16[128,256]{1,0:T(8,128)(2,1)S(1)}, bf16[128,256]{1,0:T(8,128)(2,1)}, u32[]{:S(2)}) copy-start(bf16[128,256]{1,0:T(8,128)(2,1)} %param.11) | copy-start | bytes 196612
Sparse Core Ops, SparseCore 0:
  224.9 158.2 all-reduce.3
  388.4 66.4 all-gather.1
where the time goes:
time: 535 us; the launch traced here: 533 us
  waiting for transfers between devices  382 us (71%)
  starting transfers between devices  55.9 us (10%)
  local copies, waits for them, and re-layouts  36.6 us (7%)
  matrix products  29.3 us (5%)
  between operations  14.9 us (3%)
  other arithmetic  14.2 us (3%)
    psum x1, waiting for transfers between devices, body(): pre_full = lax.psum(partial_value, 'member').astype(jnp.float32)  156 us
    all_to_all x1, waiting for transfers between devices, body(): lax.all_to_all(down_parts, 'dp', split_axis=0, concat_axis=1, tiled=True)  47.9 us
    all_to_all x1, waiting for transfers between devices, body(): lax.all_to_all(spread(d_local), 'dp', split_axis=0, concat_axis=0, tiled=...  38 us
    all_to_all x1, waiting for transfers between devices, body(): lax.all_to_all(up_parts, 'dp', split_axis=0, concat_axis=1, tiled=True)  37.2 us
    all_gather x1, waiting for transfers between devices, body(): d_pre = lax.all_gather(d_share, 'member', axis=0, tiled=True)  37 us
    all_to_all x1, waiting for transfers between devices, body(): lax.all_to_all(spread(x_local), 'dp', split_axis=0, concat_axis=0, tiled=...  36.7 us
    all_to_all x1, waiting for transfers between devices, body(): lax.all_to_all(dx_part.reshape(dp_count, CAP, features).astype(jnp.bfloat...  28.9 us
    dot_general x5, matrix products, contract(): lax.dot_general(left, right, (((left_dim,), (right_dim,)), ((), ())), pre...  22.5 us
  transfers between devices with their start and end apart: 8, of which 7 were waited for; matrix products, arithmetic and copies ran while one was open for 12% of the time, Pallas kernels for 0%

commit v1 on v0

--- a/solution.py
+++ b/solution.py
@@ -6,6 +6,14 @@
 FF_W = 7168
 E = 8
 CAP = 34
+
+
+def gather_by_exchange(value, axis, dim):
+    count = lax.axis_size(axis)
+    repeats = [count if d == dim else 1 for d in range(value.ndim)]
+    return lax.all_to_all(
+        jnp.tile(value, repeats), axis, split_axis=dim, concat_axis=dim, tiled=True
+    )
 
 
 def contract(left, right, left_dim, right_dim):
@@ -105,7 +113,7 @@
     pre_share = lax.dynamic_slice_in_dim(pre_full, own_start, per_member, 1).T
     sigma = jax.nn.sigmoid(pre_share)
     d_share = (d_act * sigma * (1.0 + pre_share * (1.0 - sigma))).astype(jnp.bfloat16)
-    d_pre = lax.all_gather(d_share, "member", axis=0, tiled=True)
+    d_pre = gather_by_exchange(d_share, "member", 0)
     g_down = contract(d_in, act_full, 0, 0)
     g_up = contract(x_in, d_pre, 0, 1)
     dx_part = contract(d_pre, up_own, 0, 1)

time: 535 us -> 563 us (1.052)
  waiting for transfers between devices: 382 us -> 411 us
    all_to_all x0 -> x1, waiting for transfers between devices: none -> 44.9 us  [gather_by_exchange(): lax.all_to_all(jnp.tile(value, repeats), axis, split_axis=dim, concat_axi...]
    all_gather x1 -> x0, waiting for transfers between devices: 37 us -> none  [body(): d_pre = lax.all_gather(d_share, 'member', axis=0, tiled=True)]
    all_to_all x1, waiting for transfers between devices: 0.01 us -> 21 us  [body(): lax.all_to_all(y_part.reshape(dp_count, CAP, features).astype(jnp.bfloat1...]
    all_to_all x1, starting transfers between devices: 13 us -> 4.06 us  [body(): lax.all_to_all(dx_part.reshape(dp_count, CAP, features).astype(jnp.bfloat...]
  transfers between devices with their start and end apart: 8 -> 8, of which waited for: 7 -> 8; matrix products, arithmetic and copies ran while one was open for 12% -> 12% of each run, Pallas kernels for 0% -> 0%
where the time goes in v1:
time: 563 us; the launch traced here: 561 us
  waiting for transfers between devices  411 us (73%)
  starting transfers between devices  53.2 us (9%)
  local copies, waits for them, and re-layouts  38.1 us (7%)
  matrix products  29.4 us (5%)
  between operations  14.9 us (3%)
  other arithmetic  14.2 us (3%)
    psum x1, waiting for transfers between devices, body(): pre_full = lax.psum(partial_value, 'member').astype(jnp.float32)  156 us
    all_to_all x1, waiting for transfers between devices, body(): lax.all_to_all(down_parts, 'dp', split_axis=0, concat_axis=1, tiled=True)  47.9 us
    all_to_all x1, waiting for transfers between devices, gather_by_exchange(): lax.all_to_all(jnp.tile(value, repeats), axis, split_axis=dim, concat_axi...  44.9 us
    all_to_all x1, waiting for transfers between devices, body(): lax.all_to_all(spread(d_local), 'dp', split_axis=0, concat_axis=0, tiled=...  38 us
    all_to_all x1, waiting for transfers between devices, body(): lax.all_to_all(up_parts, 'dp', split_axis=0, concat_axis=1, tiled=True)  37.2 us
    all_to_all x1, waiting for transfers between devices, body(): lax.all_to_all(spread(x_local), 'dp', split_axis=0, concat_axis=0, tiled=...  36.7 us
    all_to_all x1, waiting for transfers between devices, body(): lax.all_to_all(dx_part.reshape(dp_count, CAP, features).astype(jnp.bfloat...  28.8 us
    dot_general x5, matrix products, contract(): lax.dot_general(left, right, (((left_dim,), (right_dim,)), ((), ())), pre...  22.6 us
  transfers between devices with their start and end apart: 8, of which 8 were waited for; matrix products, arithmetic and copies ran while one was open for 12% of the time, Pallas kernels for 0%

profile of v1, /device:TPU:1, one launch (start us, length us, event | category | flops | bytes accessed | tf_op | source)
XLA Modules:
  0.0 560.9 jit_solution(8641395452522870192)
XLA Ops:
  11.4 16.7 %all-to-all-start.4 = ((bf16[32,34,256]{2,1,0:T(8,128)(2,1)}), bf16[32,34,256]{2,1,0:T(8,128)(2,1)S(1)}, u32[]{:S(2)}, u32[]{:S(2)}) async-start(bf16[32,34,256]{2,1,0:T(8,128)(2,1)} %bitcast.7), calls=%async_computation.4 | async-start | bytes 1310720 | tf_op jit(solution)/shard_map/all_to_all | solution.py:103
  29.2 38.0 %all-to-all-done.4 = bf16[32,34,256]{2,1,0:T(8,128)(2,1)S(1)} async-done(((bf16[32,34,256]{2,1,0:T(8,128)(2,1)}), bf16[32,34,256]{2,1,0:T(8,128)(2,1)S(1)}, u32[]{:S(2)}, u32[]{:S(2)}) %all-to-all-start.4) | async-done | bytes 557088 | tf_op jit(solution)/shard_map/all_to_all | solution.py:103
  68.1 4.1 all-to-all-start
  72.2 1.3 fusion.14
  74.6 36.7 %all-to-all-done = bf16[32,34,256]{2,1,0:T(8,128)(2,1)S(1)} async-done(((bf16[32,34,256]{2,1,0:T(8,128)(2,1)}), bf16[32,34,256]{2,1,0:T(8,128)(2,1)S(1)}, u32[]{:S(2)}, u32[]{:S(2)}) %all-to-all-start) | async-done | bytes 557088 | tf_op jit(solution)/shard_map/all_to_all | solution.py:88
  112.1 4.5 all-to-all-start.2
  116.6 1.3 fusion.15
  118.9 47.9 %all-to-all-done.2 = bf16[32,8,1792]{2,1,0:T(8,128)(2,1)S(1)} async-done(((bf16[32,8,1792]{2,1,0:T(8,128)(2,1)}), bf16[32,8,1792]{2,1,0:T(8,128)(2,1)S(1)}, u32[]{:S(2)}, u32[]{:S(2)}) %all-to-all-start.2) | async-done | bytes 917536 | tf_op jit(solution)/shard_map/all_to_all | solution.py:46
  166.9 4.5 all-to-all-start.1
  173.7 4.4 convolution_convert_fusion
  178.1 6.4 %copy.29 = bf16[1792,1088]{0,1:T(8,128)(2,1)} copy(bf16[1792,1088]{1,0:T(8,128)(2,1)} %convolution_convert_fusion) | data formatting | bytes 7798784 | tf_op jit(solution)/shard_map/convert_element_type | solution.py:107
  184.5 37.2 %all-to-all-done.1 = bf16[32,8,1792]{2,1,0:T(8,128)(2,1)S(1)} async-done(((bf16[32,8,1792]{2,1,0:T(8,128)(2,1)}), bf16[32,8,1792]{2,1,0:T(8,128)(2,1)S(1)}, u32[]{:S(2)}, u32[]{:S(2)}) %all-to-all-start.1) | async-done | bytes 917536 | tf_op jit(solution)/shard_map/all_to_all | solution.py:45
  221.7 3.1 convolution_convert_fusion.1
  224.8 1.3 dynamic-slice
  226.7 156.5 %all-reduce.4.cloned.1.call-done = (bf16[1088,1792]{1,0:T(8,128)(2,1)}, bf16[1792,1088]{0,1:T(8,128)(2,1)}) async-done(((bf16[1088,1792]{1,0:T(8,128)(2,1)}, bf16[1792,1088]{0,1:T(8,128)(2,1)}), (bf16[1088,1792]{1,0:T(8,128)(2,1)}, bf16[1792,1088]{0,1:T(8,128)(2,1)})) %all-reduce.4.cloned.1.call-update) | async-done | bytes 7798800 | tf_op jit(solution)/shard_map/psum | solution.py:92
  383.2 2.7 convert_element_type.68
  385.9 1.4 fusion.11
  387.5 2.2 tile.2
  389.8 5.1 all-to-all-start.5
  394.9 5.0 multiply_convert_fusion
  400.0 6.9 %dot_general.42 = bf16[32,34,1792]{2,1,0:T(8,128)(2,1)} reshape(bf16[1088,1792]{1,0:T(8,128)(2,1)} %multiply_convert_fusion) | data formatting | bytes 7798784 | tf_op jit(solution)/shard_map/dot_general | solution.py:20
  406.9 4.6 convolution_convert_fusion.5
  411.5 44.9 %all-to-all-done.5 = bf16[16,112,1088]{2,1,0:T(8,128)(2,1)} async-done(((bf16[16,112,1088]{2,1,0:T(8,128)(2,1)}), bf16[16,112,1088]{2,1,0:T(8,128)(2,1)}, u32[]{:S(2)}, u32[]{:S(2)}) %all-to-all-start.5) | async-done | bytes 3899424 | tf_op jit(solution)/shard_map/all_to_all | solution.py:14
  456.4 14.2 %all-to-all-start.3 = ((bf16[32,34,256]{2,1,0:T(8,128)(2,1)}), bf16[32,34,256]{2,1,0:T(8,128)(2,1)S(1)}, u32[]{:S(2)}, u32[]{:S(2)}) async-start(bf16[32,34,256]{2,1,0:T(8,128)(2,1)} %convolution_convert_fusion.5), calls=%async_computation.3 | async-start | bytes 1310720 | tf_op jit(solution)/shard_map/all_to_all | solution.py:96
  470.5 6.4 %copy.31 = bf16[1088,1792]{1,0:T(8,128)(2,1)} copy(bf16[1088,1792]{0,1:T(8,128)(2,1)} %bitcast.10) | data formatting | bytes 7798784 | tf_op jit(solution)/shard_map/dot_general | solution.py:20
  476.9 6.9 %dot_general.48 = bf16[32,34,1792]{2,1,0:T(8,128)(2,1)} reshape(bf16[1088,1792]{1,0:T(8,128)(2,1)} %copy.31) | data formatting | bytes 7798784 | tf_op jit(solution)/shard_map/dot_general | solution.py:20
  483.9 4.7 convolution_convert_fusion.4
  488.6 21.0 %all-to-all-done.3 = bf16[32,34,256]{2,1,0:T(8,128)(2,1)S(1)} async-done(((bf16[32,34,256]{2,1,0:T(8,128)(2,1)}), bf16[32,34,256]{2,1,0:T(8,128)(2,1)S(1)}, u32[]{:S(2)}, u32[]{:S(2)}) %all-to-all-start.3) | async-done | bytes 557088 | tf_op jit(solution)/shard_map/all_to_all | solution.py:96
  509.6 4.1 all-to-all-start.6
  513.7 4.4 fusion.1
  519.4 4.5 fusion
  523.9 28.8 %all-to-all-done.6 = bf16[32,34,256]{2,1,0:T(8,128)(2,1)S(1)} async-done(((bf16[32,34,256]{2,1,0:T(8,128)(2,1)}), bf16[32,34,256]{2,1,0:T(8,128)(2,1)S(1)}, u32[]{:S(2)}, u32[]{:S(2)}) %all-to-all-start.6) | async-done | bytes 557088 | tf_op jit(solution)/shard_map/all_to_all | solution.py:121
  (32 shorter events, 14.0 us)
Async XLA Ops:
  7.2 3.0 copy-start
  11.4 55.9 %all-to-all-start.4 = ((bf16[32,34,256]{2,1,0:T(8,128)(2,1)}), bf16[32,34,256]{2,1,0:T(8,128)(2,1)S(1)}, u32[]{:S(2)}, u32[]{:S(2)}) async-start(bf16[32,34,256]{2,1,0:T(8,128)(2,1)} %bitcast.7), calls=%async_computation.4 | async-start | bytes 1310720 | tf_op jit(solution)/shard_map/all_to_all | solution.py:103
  68.1 43.1 %all-to-all-start = ((bf16[32,34,256]{2,1,0:T(8,128)(2,1)}), bf16[32,34,256]{2,1,0:T(8,128)(2,1)S(1)}, u32[]{:S(2)}, u32[]{:S(2)}) async-start(bf16[32,34,256]{2,1,0:T(8,128)(2,1)} %bitcast), calls=%async_computation | async-start | bytes 1310720 | tf_op jit(solution)/shard_map/all_to_all | solution.py:88
  111.3 0.8 copy-start.2
  112.1 54.7 %all-to-all-start.2 = ((bf16[32,8,1792]{2,1,0:T(8,128)(2,1)}), bf16[32,8,1792]{2,1,0:T(8,128)(2,1)S(1)}, u32[]{:S(2)}, u32[]{:S(2)}) async-start(bf16[32,8,1792]{2,1,0:T(8,128)(2,1)} %bitcast.3), calls=%async_computation.2 | async-start | bytes 1835008 | tf_op jit(solution)/shard_map/all_to_all | solution.py:46
  166.9 54.8 %all-to-all-start.1 = ((bf16[32,8,1792]{2,1,0:T(8,128)(2,1)}), bf16[32,8,1792]{2,1,0:T(8,128)(2,1)S(1)}, u32[]{:S(2)}, u32[]{:S(2)}) async-start(bf16[32,8,1792]{2,1,0:T(8,128)(2,1)} %bitcast.1), calls=%async_computation.1 | async-start | bytes 1835008 | tf_op jit(solution)/shard_map/all_to_all | solution.py:45
  171.4 211.8 %all-reduce.4.cloned.1.call-start = ((), (), s32[]{:S(2)}) async-start(), calls=%async_computation.7 | async-start | bytes 15597568 | tf_op jit(solution)/shard_map/psum | solution.py:92
  389.8 66.6 %all-to-all-start.5 = ((bf16[16,112,1088]{2,1,0:T(8,128)(2,1)}), bf16[16,112,1088]{2,1,0:T(8,128)(2,1)}, u32[]{:S(2)}, u32[]{:S(2)}) async-start(bf16[16,112,1088]{2,1,0:T(8,128)(2,1)} %tile.2), calls=%async_computation.5 | async-start | bytes 8257536 | tf_op jit(solution)/shard_map/all_to_all | solution.py:14
  456.4 53.3 %all-to-all-start.3 = ((bf16[32,34,256]{2,1,0:T(8,128)(2,1)}), bf16[32,34,256]{2,1,0:T(8,128)(2,1)S(1)}, u32[]{:S(2)}, u32[]{:S(2)}) async-start(bf16[32,34,256]{2,1,0:T(8,128)(2,1)} %convolution_convert_fusion.5), calls=%async_computation.3 | async-start | bytes 1310720 | tf_op jit(solution)/shard_map/all_to_all | solution.py:96
  483.9 29.8 %copy-start.3 = (bf16[1088,256]{1,0:T(8,128)(2,1)S(1)}, bf16[1088,256]{1,0:T(8,128)(2,1)}, u32[]{:S(2)}) copy-start(bf16[1088,256]{1,0:T(8,128)(2,1)} %reshape.95) | copy-start | bytes 1671172
  509.6 43.1 %all-to-all-start.6 = ((bf16[32,34,256]{2,1,0:T(8,128)(2,1)}), bf16[32,34,256]{2,1,0:T(8,128)(2,1)S(1)}, u32[]{:S(2)}, u32[]{:S(2)}) async-start(bf16[32,34,256]{2,1,0:T(8,128)(2,1)} %convolution_convert_fusion.4), calls=%async_computation.6 | async-start | bytes 1310720 | tf_op jit(solution)/shard_map/all_to_all | solution.py:121
  519.4 34.7 %copy-start.1 = (bf16[128,256]{1,0:T(8,128)(2,1)S(1)}, bf16[128,256]{1,0:T(8,128)(2,1)}, u32[]{:S(2)}) copy-start(bf16[128,256]{1,0:T(8,128)(2,1)} %param.11) | copy-start | bytes 196612
Sparse Core Ops, SparseCore 0:
  224.9 158.2 all-reduce.3
